TPU v7x, 32 devices: a whole 2x2x4 slice. The times are simulated.
32 devices in a mesh: rows: 8 (over z, core), pairs: 4 (over y, x).
Axes of the slice: x: 2, y: 2, z: 4, core: 2. Of those that a mesh axis runs over, the one named last changes fastest.
Arguments:
- observed: float32 [12288, 2048], P('rows', 'pairs'), as said below
- estimate: float32 [12288, 2048], P('rows', 'pairs'), may hold values from -0.054126587 to 0.054126587
- mask: int32 [12288, 2048], P('rows', 'pairs'), may hold values from 0 to 1
- threshold: float32 [2048], P('pairs'), may hold values from 0.02 to 0.12
Outputs:
- regrouped: float32 [2048, 12288], P(('rows', 'pairs'))
Inputs may be any that keep to these rules, and one draw needn't show every extreme that they name: observed has entries of order 12288^-1/2.
All inputs are finite; a program needn't handle non-finite values.
Results may differ from a plain program's by a relative error of at most 0.0003.
Values sent between devices are 32-bit elements; how exact they have to be, the bound alone decides.
A program may use at most 128 MiB of HBM per device.

v0:
```python
import jax
import jax.numpy as jnp
from jax import lax
from jax.sharding import PartitionSpec as P

ROUNDS = 4
NS_STEPS = 3
HI = lax.Precision.HIGHEST


def from_behind(block, axis, distance):
    devices = range(lax.axis_size(axis))
    route = [((i - distance) % len(devices), i) for i in devices]
    return lax.ppermute(block, axis, route)


def whitening_of(gram):
    width = gram.shape[-1]
    eye = jnp.eye(width, dtype=jnp.float32)
    dsum = jnp.diagonal(gram, axis1=-2, axis2=-1) + 1e-06
    inv_root = 1.0 / jnp.sqrt(dsum)
    normed = gram * inv_root[..., :, None] * inv_root[..., None, :]
    fro = jnp.sqrt(jnp.sum(normed * normed, axis=(-2, -1)))
    ymat = normed / fro[..., None, None]
    zmat = jnp.broadcast_to(eye, normed.shape)
    for step in range(NS_STEPS):
        tmat = 1.5 * eye - 0.5 * jnp.einsum("pij,pjk->pik", zmat, ymat, precision=HI)
        ymat = jnp.einsum("pij,pjk->pik", ymat, tmat, precision=HI)
        zmat = jnp.einsum("pij,pjk->pik", tmat, zmat, precision=HI)
    return (
        inv_root[..., :, None]
        * zmat
        * jnp.sqrt(dsum)[..., None, :]
        / jnp.sqrt(fro)[..., None, None]
    )


def on_device(observed, estimate, mask, threshold):
    filled = jnp.where(mask == 1, observed, estimate)
    rows_here, width = filled.shape
    block = width // 4
    for round_index in range(ROUNDS):
        pairs = filled.reshape(rows_here, 2, 2 * block)
        partial_gram = jnp.einsum("rpi,rpj->pij", pairs, pairs, precision=HI)
        gram = lax.psum(partial_gram, "rows")
        whitening = whitening_of(gram)
        pairs = jnp.einsum("rpi,pij->rpj", pairs, whitening, precision=HI)
        quads = pairs.reshape(rows_here, 4, block)
        if round_index + 1 < ROUNDS:
            moved = from_behind(quads[:, 3], "pairs", 1)
            quads = jnp.stack([quads[:, 0], moved, quads[:, 2], quads[:, 1]], axis=1)
        filled = quads.reshape(rows_here, width)
    squares = lax.psum(jnp.sum(filled * filled, axis=0), "rows")
    col_norm = jnp.sqrt(squares + 1e-06)
    factor = jnp.maximum(col_norm - threshold, 0.0) / col_norm
    shrunk_t = (filled * factor[None, :]).T
    count_rows = lax.axis_size("rows")
    count_pairs = lax.axis_size("pairs")
    each_dest = width // (count_rows * count_pairs)
    packed = shrunk_t.reshape(count_rows * count_pairs, each_dest, rows_here)
    landed = lax.all_to_all(packed, ("rows", "pairs"), split_axis=0, concat_axis=1, tiled=True)
    landed = landed.reshape(count_rows, count_pairs, each_dest, rows_here).transpose(2, 1, 0, 3)
    return landed.reshape(each_dest * count_pairs, count_rows * rows_here)


def solution(mesh):
    placed = (P("rows", "pairs"), P("rows", "pairs"), P("rows", "pairs"), P("pairs"))
    return jax.shard_map(
        on_device, mesh=mesh, in_specs=placed, out_specs=P(("rows", "pairs"), None), check_vma=False
    )
```

profile of v0, /device:TPU:0, one launch (start us, length us, event | category | flops | bytes accessed | tf_op | source)
XLA Modules:
  0.0 571.2 jit_solution(13144928827066859881)
XLA Ops:
  6.5 4.9 compare_select_fusion
  11.4 6.2 %fusion.2 = f32[2,256,256]{2,1,0:T(8,128)} fusion(f32[192,2,8,256]{3,2,1,0:T(8,128)S(1)} %bitcast.133), kind=kOutput, calls=%fused_computation.6 | convolution fusion | flops 2415919104 | bytes 3670016 | tf_op jit(solution)/shard_map/rpi,rpj->pij/dot_general | solution.py:44
  18.5 58.6 %all-reduce.5.cloned.1.call-done = f32[2,256,256]{2,1,0:T(8,128)} async-done(((f32[2,256,256]{2,1,0:T(8,128)}), f32[2,256,256]{2,1,0:T(8,128)}) %all-reduce.5.cloned.1.call-update) | async-done | bytes 524304 | tf_op jit(solution)/shard_map/psum | solution.py:45
  77.0 17.5 %copy.62 = f32[2,256,256]{0,2,1:T(8,128)} copy(f32[2,256,256]{2,1,0:T(8,128)} %all-reduce.5.cloned.1.call-done) | data formatting | bytes 1048576 | tf_op jit(solution)/shard_map/psum | solution.py:45
  94.5 3.0 gather_fusion
  101.5 1.9 fusion.26
  112.0 5.3 fusion
  119.1 16.9 %collective-permute-done = f32[1536,128]{0,1:T(8,128)S(1)} collective-permute-done((f32[1536,128]{0,1:T(8,128)S(1)}, f32[1536,128]{0,1:T(8,128)S(1)}, u32[]{:S(2)}, u32[]{:S(2)}) %collective-permute-start) | collective-permute-done | bytes 786464 | tf_op jit(solution)/shard_map/ppermute | solution.py:14
  136.4 3.9 fusion.62
  140.8 55.3 %all-reduce.7.cloned.1.call-done = f32[2,256,256]{2,1,0:T(8,128)} async-done(((f32[2,256,256]{2,1,0:T(8,128)}), f32[2,256,256]{2,1,0:T(8,128)}) %all-reduce.7.cloned.1.call-update) | async-done | bytes 524304 | tf_op jit(solution)/shard_map/psum | solution.py:45
  196.0 17.3 %copy.69 = f32[2,256,256]{0,2,1:T(8,128)} copy(f32[2,256,256]{2,1,0:T(8,128)} %all-reduce.7.cloned.1.call-done) | data formatting | bytes 1048576 | tf_op jit(solution)/shard_map/psum | solution.py:45
  213.3 3.0 gather_fusion.1
  220.2 1.9 fusion.21
  230.7 3.1 fusion.65
  235.8 16.9 %collective-permute-done.1 = f32[1536,128]{0,1:T(8,128)S(1)} collective-permute-done((f32[1536,128]{0,1:T(8,128)S(1)}, f32[1536,128]{0,1:T(8,128)S(1)}, u32[]{:S(2)}, u32[]{:S(2)}) %collective-permute-start.1) | collective-permute-done | bytes 786464 | tf_op jit(solution)/shard_map/ppermute | solution.py:14
  253.0 3.9 fusion.66
  257.0 55.7 %all-reduce.9.cloned.1.call-done = f32[2,256,256]{2,1,0:T(8,128)} async-done(((f32[2,256,256]{2,1,0:T(8,128)}), f32[2,256,256]{2,1,0:T(8,128)}) %all-reduce.9.cloned.1.call-update) | async-done | bytes 524304 | tf_op jit(solution)/shard_map/psum | solution.py:45
  312.6 17.3 %copy.76 = f32[2,256,256]{0,2,1:T(8,128)} copy(f32[2,256,256]{2,1,0:T(8,128)} %all-reduce.9.cloned.1.call-done) | data formatting | bytes 1048576 | tf_op jit(solution)/shard_map/psum | solution.py:45
  329.9 3.0 gather_fusion.2
  336.9 1.9 fusion.16
  347.4 3.1 fusion.69
  352.5 16.9 %collective-permute-done.2 = f32[1536,128]{0,1:T(8,128)S(1)} collective-permute-done((f32[1536,128]{0,1:T(8,128)S(1)}, f32[1536,128]{0,1:T(8,128)S(1)}, u32[]{:S(2)}, u32[]{:S(2)}) %collective-permute-start.2) | collective-permute-done | bytes 786464 | tf_op jit(solution)/shard_map/ppermute | solution.py:14
  369.7 3.9 fusion.70
  373.6 55.7 %all-reduce.11.cloned.1.call-done = f32[2,256,256]{2,1,0:T(8,128)} async-done(((f32[2,256,256]{2,1,0:T(8,128)}), f32[2,256,256]{2,1,0:T(8,128)}) %all-reduce.11.cloned.1.call-update) | async-done | bytes 524304 | tf_op jit(solution)/shard_map/psum | solution.py:45
  429.3 17.3 %copy.83 = f32[2,256,256]{0,2,1:T(8,128)} copy(f32[2,256,256]{2,1,0:T(8,128)} %all-reduce.11.cloned.1.call-done) | data formatting | bytes 1048576 | tf_op jit(solution)/shard_map/psum | solution.py:45
  446.6 3.0 gather_fusion.3
  453.5 1.9 fusion.11
  464.1 4.7 fusion.4
  468.8 13.7 %psum.39 = f32[512]{0:T(512)S(1)} all-reduce(f32[512]{0:T(512)S(1)} %bitcast.145), channel_id=1, replica_groups=mesh['rows'=8,'pairs'=4] {'rows'}, use_global_device_ids=true, to_apply=%region_9.10 | all-reduce | flops 512 | bytes 4096 | tf_op jit(solution)/shard_map/psum | solution.py:53
  482.5 2.2 bitcast_multiply_fusion
  484.7 74.3 %all_to_all.4 = f32[32,16,1536]{2,1,0:T(8,128)S(1)} all-to-all(f32[32,16,1536]{2,1,0:T(8,128)S(1)} %bitcast.135), channel_id=1, replica_groups=mesh['rows'=8,'pairs'=4] {'rows','pairs'}, dimensions={0} | all-to-all | bytes 6291456 | tf_op jit(solution)/shard_map/all_to_all | solution.py:61
  560.8 3.4 copy.102
  (89 shorter events, 60.0 us)
Async XLA Ops:
  6.5 70.5 %all-reduce.5.cloned.1.call-start = ((), (), s32[]{:S(2)}) async-start(), calls=%async_computation.1 | async-start | bytes 1048576 | tf_op jit(solution)/shard_map/psum | solution.py:45
  17.7 178.4 %all-reduce.7.cloned.1.call-start = ((), (), s32[]{:S(2)}) async-start(), calls=%async_computation.2 | async-start | bytes 1048576 | tf_op jit(solution)/shard_map/psum | solution.py:45
  100.1 3.3 copy-start
  100.1 3.9 copy-start.4
  117.6 18.5 %collective-permute-start = (f32[1536,128]{0,1:T(8,128)S(1)}, f32[1536,128]{0,1:T(8,128)S(1)}, u32[]{:S(2)}, u32[]{:S(2)}) collective-permute-start(f32[1536,128]{0,1:T(8,128)S(1)} %get-tuple-element.16), channel_id=1, source_target_pairs={{3,0},{0,1},{1,2},{2,3},{7,4},{4,5},{5,6},{6,7},{11,8},{8,9},{9,10... | collective-permute-start | bytes 2359304 | tf_op jit(solution)/shard_map/ppermute | solution.py:14
  140.2 172.4 %all-reduce.9.cloned.1.call-start = ((), (), s32[]{:S(2)}) async-start(), calls=%async_computation.3 | async-start | bytes 1048576 | tf_op jit(solution)/shard_map/psum | solution.py:45
  218.8 3.3 copy-start.1
  218.8 3.9 copy-start.5
  234.1 18.6 %collective-permute-start.1 = (f32[1536,128]{0,1:T(8,128)S(1)}, f32[1536,128]{0,1:T(8,128)S(1)}, u32[]{:S(2)}, u32[]{:S(2)}) collective-permute-start(f32[1536,128]{0,1:T(8,128)S(1)} %get-tuple-element.12), channel_id=1, source_target_pairs={{3,0},{0,1},{1,2},{2,3},{7,4},{4,5},{5,6},{6,7},{11,8},{8,9},{9,10... | collective-permute-start | bytes 2359304 | tf_op jit(solution)/shard_map/ppermute | solution.py:14
  256.9 172.4 %all-reduce.11.cloned.1.call-start = ((), (), s32[]{:S(2)}) async-start(), calls=%async_computation.4 | async-start | bytes 1048576 | tf_op jit(solution)/shard_map/psum | solution.py:45
  335.5 3.3 copy-start.2
  335.5 3.9 copy-start.6
  350.7 18.7 %collective-permute-start.2 = (f32[1536,128]{0,1:T(8,128)S(1)}, f32[1536,128]{0,1:T(8,128)S(1)}, u32[]{:S(2)}, u32[]{:S(2)}) collective-permute-start(f32[1536,128]{0,1:T(8,128)S(1)} %get-tuple-element.8), channel_id=1, source_target_pairs={{3,0},{0,1},{1,2},{2,3},{7,4},{4,5},{5,6},{6,7},{11,8},{8,9},{9,10... | collective-permute-start | bytes 2359304 | tf_op jit(solution)/shard_map/ppermute | solution.py:14
  452.1 3.3 copy-start.3
  452.1 3.9 copy-start.7
  464.0 18.4 %copy-start.8 = (f32[512]{0:T(512)S(1)}, f32[512]{0:T(512)}, u32[]{:S(2)}) copy-start(f32[512]{0:T(512)} %param.7) | copy-start | bytes 6148
Sparse Core Ops, SparseCore 0:
  17.8 59.2 all-reduce.4
  140.4 55.6 all-reduce.6
  257.0 55.5 all-reduce.8
  373.7 55.5 all-reduce.10
where the time goes:
time: 579 us; the launch traced here: 571 us
  waiting for transfers between devices  276 us (48%)
  local copies, waits for them, and re-layouts  91.6 us (16%)
  blocking collectives  88 us (15%)
  matrix products  75.5 us (13%)
  other arithmetic  20.6 us (4%)
  between operations  14 us (2%)
    psum x4, waiting for transfers between devices, on_device(): gram = lax.psum(partial_gram, 'rows')  225 us
    all_to_all x1, blocking collectives, on_device(): lax.all_to_all(packed, ('rows', 'pairs'), split_axis=0, concat_axis=1, ti...  74.3 us
    psum x4, local copies, waits for them, and re-layouts, on_device(): gram = lax.psum(partial_gram, 'rows')  69.3 us
    ppermute x3, waiting for transfers between devices, from_behind(): return lax.ppermute(block, axis, route)  50.8 us
    dot_general x4, matrix products, on_device(): partial_gram = jnp.einsum('rpi,rpj->pij', pairs, pairs, precision=HI)  17.7 us
    dot_general x12, matrix products, whitening_of(): jnp.einsum('pij,pjk->pik', zmat, ymat, precision=HI)  17.6 us
    dot_general x4, matrix products, on_device(): pairs = jnp.einsum('rpi,pij->rpj', pairs, whitening, precision=HI)  16.3 us
    dot_general x12, matrix products, whitening_of(): zmat = jnp.einsum('pij,pjk->pik', tmat, zmat, precision=HI)  15.2 us
  transfers between devices with their start and end apart: 7, of which 7 were waited for; matrix products, arithmetic and copies ran while one was open for 0% of the time, Pallas kernels for 0%

commit v1 on v0

--- a/solution.py
+++ b/solution.py
@@ -58,7 +58,15 @@
     count_pairs = lax.axis_size("pairs")
     each_dest = width // (count_rows * count_pairs)
     packed = shrunk_t.reshape(count_rows * count_pairs, each_dest, rows_here)
-    landed = lax.all_to_all(packed, ("rows", "pairs"), split_axis=0, concat_axis=1, tiled=True)
+    landed = jnp.concatenate(
+        lax.all_to_all(
+            jnp.stack(jnp.split(packed, lax.axis_size(("rows", "pairs")), axis=0)),
+            ("rows", "pairs"),
+            0,
+            0,
+        ),
+        axis=1,
+    )
     landed = landed.reshape(count_rows, count_pairs, each_dest, rows_here).transpose(2, 1, 0, 3)
     return landed.reshape(each_dest * count_pairs, count_rows * rows_here)
 

time: 579 us -> 579 us (level)
  no operation moved by 1% of the time
where the time goes in v1:
time: 579 us; the launch traced here: 571 us
  waiting for transfers between devices  276 us (48%)
  local copies, waits for them, and re-layouts  91.6 us (16%)
  blocking collectives  88 us (15%)
  matrix products  75.7 us (13%)
  other arithmetic  20.3 us (4%)
  between operations  14.2 us (2%)
    psum x4, waiting for transfers between devices, on_device(): gram = lax.psum(partial_gram, 'rows')  225 us
    all_to_all x1, blocking collectives, on_device(): lax.all_to_all(jnp.stack(jnp.split(packed, lax.axis_size(('rows', 'pairs'...  74.3 us
    psum x4, local copies, waits for them, and re-layouts, on_device(): gram = lax.psum(partial_gram, 'rows')  69.3 us
    ppermute x3, waiting for transfers between devices, from_behind(): return lax.ppermute(block, axis, route)  50.8 us
    dot_general x4, matrix products, on_device(): partial_gram = jnp.einsum('rpi,rpj->pij', pairs, pairs, precision=HI)  17.8 us
    dot_general x12, matrix products, whitening_of(): jnp.einsum('pij,pjk->pik', zmat, ymat, precision=HI)  17.7 us
    dot_general x4, matrix products, on_device(): pairs = jnp.einsum('rpi,pij->rpj', pairs, whitening, precision=HI)  16.3 us
    dot_general x12, matrix products, whitening_of(): zmat = jnp.einsum('pij,pjk->pik', tmat, zmat, precision=HI)  15.3 us
  transfers between devices with their start and end apart: 7, of which 7 were waited for; matrix products, arithmetic and copies ran while one was open for 0% of the time, Pallas kernels for 0%

profile of v1, /device:TPU:0, one launch (start us, length us, event | category | flops | bytes accessed | tf_op | source)
XLA Modules:
  0.0 571.5 jit_solution(684438693749981556)
XLA Ops:
  6.5 4.9 compare_select_fusion
  11.4 6.2 %fusion.2 = f32[2,256,256]{2,1,0:T(8,128)} fusion(f32[192,2,8,256]{3,2,1,0:T(8,128)S(1)} %bitcast.258), kind=kOutput, calls=%fused_computation.6 | convolution fusion | flops 2415919104 | bytes 3670016 | tf_op jit(solution)/shard_map/rpi,rpj->pij/dot_general | solution.py:44
  18.5 58.6 %all-reduce.5.cloned.1.call-done = f32[2,256,256]{2,1,0:T(8,128)} async-done(((f32[2,256,256]{2,1,0:T(8,128)}), f32[2,256,256]{2,1,0:T(8,128)}) %all-reduce.5.cloned.1.call-update) | async-done | bytes 524304 | tf_op jit(solution)/shard_map/psum | solution.py:45
  77.1 17.5 %copy.34 = f32[2,256,256]{0,2,1:T(8,128)} copy(f32[2,256,256]{2,1,0:T(8,128)} %all-reduce.5.cloned.1.call-done) | data formatting | bytes 1048576 | tf_op jit(solution)/shard_map/psum | solution.py:45
  94.5 3.0 gather_fusion
  101.5 1.9 fusion.26
  112.0 5.4 fusion
  119.1 16.9 %collective-permute-done = f32[1536,128]{0,1:T(8,128)S(1)} collective-permute-done((f32[1536,128]{0,1:T(8,128)S(1)}, f32[1536,128]{0,1:T(8,128)S(1)}, u32[]{:S(2)}, u32[]{:S(2)}) %collective-permute-start) | collective-permute-done | bytes 786464 | tf_op jit(solution)/shard_map/ppermute | solution.py:14
  136.3 3.9 fusion.94
  140.7 55.3 %all-reduce.7.cloned.1.call-done = f32[2,256,256]{2,1,0:T(8,128)} async-done(((f32[2,256,256]{2,1,0:T(8,128)}), f32[2,256,256]{2,1,0:T(8,128)}) %all-reduce.7.cloned.1.call-update) | async-done | bytes 524304 | tf_op jit(solution)/shard_map/psum | solution.py:45
  195.9 17.3 %copy.41 = f32[2,256,256]{0,2,1:T(8,128)} copy(f32[2,256,256]{2,1,0:T(8,128)} %all-reduce.7.cloned.1.call-done) | data formatting | bytes 1048576 | tf_op jit(solution)/shard_map/psum | solution.py:45
  213.2 3.0 gather_fusion.1
  220.1 1.9 fusion.21
  230.7 3.1 fusion.97
  235.7 16.9 %collective-permute-done.1 = f32[1536,128]{0,1:T(8,128)S(1)} collective-permute-done((f32[1536,128]{0,1:T(8,128)S(1)}, f32[1536,128]{0,1:T(8,128)S(1)}, u32[]{:S(2)}, u32[]{:S(2)}) %collective-permute-start.1) | collective-permute-done | bytes 786464 | tf_op jit(solution)/shard_map/ppermute | solution.py:14
  252.8 3.9 fusion.98
  256.8 55.7 %all-reduce.9.cloned.1.call-done = f32[2,256,256]{2,1,0:T(8,128)} async-done(((f32[2,256,256]{2,1,0:T(8,128)}), f32[2,256,256]{2,1,0:T(8,128)}) %all-reduce.9.cloned.1.call-update) | async-done | bytes 524304 | tf_op jit(solution)/shard_map/psum | solution.py:45
  312.4 17.3 %copy.48 = f32[2,256,256]{0,2,1:T(8,128)} copy(f32[2,256,256]{2,1,0:T(8,128)} %all-reduce.9.cloned.1.call-done) | data formatting | bytes 1048576 | tf_op jit(solution)/shard_map/psum | solution.py:45
  329.7 3.0 gather_fusion.2
  336.7 1.9 fusion.16
  347.2 3.1 fusion.101
  352.2 16.9 %collective-permute-done.2 = f32[1536,128]{0,1:T(8,128)S(1)} collective-permute-done((f32[1536,128]{0,1:T(8,128)S(1)}, f32[1536,128]{0,1:T(8,128)S(1)}, u32[]{:S(2)}, u32[]{:S(2)}) %collective-permute-start.2) | collective-permute-done | bytes 786464 | tf_op jit(solution)/shard_map/ppermute | solution.py:14
  369.4 3.9 fusion.102
  373.3 55.7 %all-reduce.11.cloned.1.call-done = f32[2,256,256]{2,1,0:T(8,128)} async-done(((f32[2,256,256]{2,1,0:T(8,128)}), f32[2,256,256]{2,1,0:T(8,128)}) %all-reduce.11.cloned.1.call-update) | async-done | bytes 524304 | tf_op jit(solution)/shard_map/psum | solution.py:45
  429.0 17.3 %copy.55 = f32[2,256,256]{0,2,1:T(8,128)} copy(f32[2,256,256]{2,1,0:T(8,128)} %all-reduce.11.cloned.1.call-done) | data formatting | bytes 1048576 | tf_op jit(solution)/shard_map/psum | solution.py:45
  446.3 3.0 gather_fusion.3
  453.2 1.9 fusion.11
  463.8 4.7 fusion.4
  468.5 13.7 %psum.39 = f32[512]{0:T(512)S(1)} all-reduce(f32[512]{0:T(512)S(1)} %bitcast.301), channel_id=1, replica_groups=mesh['rows'=8,'pairs'=4] {'rows'}, use_global_device_ids=true, to_apply=%region_9.10 | all-reduce | flops 512 | bytes 4096 | tf_op jit(solution)/shard_map/psum | solution.py:53
  482.2 2.2 bitcast_multiply_fusion
  484.9 74.3 %all_to_all.5 = f32[32,1,16,1536]{3,2,1,0:T(8,128)S(1)} all-to-all(f32[32,1,16,1536]{3,2,1,0:T(8,128)S(1)} %fusion.45), channel_id=1, replica_groups=mesh['rows'=8,'pairs'=4] {'rows','pairs'}, dimensions={0} | all-to-all | bytes 6291456 | tf_op jit(solution)/shard_map/all_to_all | solution.py:62
  561.1 3.4 copy.74
  (121 shorter events, 60.0 us)
Async XLA Ops:
  6.5 70.5 %all-reduce.5.cloned.1.call-start = ((), (), s32[]{:S(2)}) async-start(), calls=%async_computation.1 | async-start | bytes 1048576 | tf_op jit(solution)/shard_map/psum | solution.py:45
  17.7 178.3 %all-reduce.7.cloned.1.call-start = ((), (), s32[]{:S(2)}) async-start(), calls=%async_computation.2 | async-start | bytes 1048576 | tf_op jit(solution)/shard_map/psum | solution.py:45
  100.1 3.3 copy-start
  100.1 3.9 copy-start.4
  117.6 18.5 %collective-permute-start = (f32[1536,128]{0,1:T(8,128)S(1)}, f32[1536,128]{0,1:T(8,128)S(1)}, u32[]{:S(2)}, u32[]{:S(2)}) collective-permute-start(f32[1536,128]{0,1:T(8,128)S(1)} %get-tuple-element.16), channel_id=1, source_target_pairs={{3,0},{0,1},{1,2},{2,3},{7,4},{4,5},{5,6},{6,7},{11,8},{8,9},{9,10... | collective-permute-start | bytes 2359304 | tf_op jit(solution)/shard_map/ppermute | solution.py:14
  140.1 172.3 %all-reduce.9.cloned.1.call-start = ((), (), s32[]{:S(2)}) async-start(), calls=%async_computation.3 | async-start | bytes 1048576 | tf_op jit(solution)/shard_map/psum | solution.py:45
  218.7 3.3 copy-start.1
  218.7 3.9 copy-start.5
  234.0 18.6 %collective-permute-start.1 = (f32[1536,128]{0,1:T(8,128)S(1)}, f32[1536,128]{0,1:T(8,128)S(1)}, u32[]{:S(2)}, u32[]{:S(2)}) collective-permute-start(f32[1536,128]{0,1:T(8,128)S(1)} %get-tuple-element.12), channel_id=1, source_target_pairs={{3,0},{0,1},{1,2},{2,3},{7,4},{4,5},{5,6},{6,7},{11,8},{8,9},{9,10... | collective-permute-start | bytes 2359304 | tf_op jit(solution)/shard_map/ppermute | solution.py:14
  256.7 172.3 %all-reduce.11.cloned.1.call-start = ((), (), s32[]{:S(2)}) async-start(), calls=%async_computation.4 | async-start | bytes 1048576 | tf_op jit(solution)/shard_map/psum | solution.py:45
  335.2 3.3 copy-start.2
  335.3 3.9 copy-start.6
  350.5 18.7 %collective-permute-start.2 = (f32[1536,128]{0,1:T(8,128)S(1)}, f32[1536,128]{0,1:T(8,128)S(1)}, u32[]{:S(2)}, u32[]{:S(2)}) collective-permute-start(f32[1536,128]{0,1:T(8,128)S(1)} %get-tuple-element.8), channel_id=1, source_target_pairs={{3,0},{0,1},{1,2},{2,3},{7,4},{4,5},{5,6},{6,7},{11,8},{8,9},{9,10... | collective-permute-start | bytes 2359304 | tf_op jit(solution)/shard_map/ppermute | solution.py:14
  451.8 3.3 copy-start.3
  451.8 3.9 copy-start.7
  463.8 18.4 %copy-start.8 = (f32[512]{0:T(512)S(1)}, f32[512]{0:T(512)}, u32[]{:S(2)}) copy-start(f32[512]{0:T(512)} %param.7) | copy-start | bytes 6148
Sparse Core Ops, SparseCore 0:
  17.8 59.2 all-reduce.4
  140.3 55.6 all-reduce.6
  256.8 55.5 all-reduce.8
  373.4 55.5 all-reduce.10
